TPU v7x, 512 devices: a whole 4x4x16 slice. The times are simulated.
512 devices in a mesh: section: 32 (over y, x, core), ctx: 16 (over z).
Axes of the slice: x: 4, y: 4, z: 16, core: 2. Of those that a mesh axis runs over, the one named last changes fastest.
Arguments:
- streams: bfloat16 [32, 2048, 5120], P('section', 'ctx'), may hold values from -6 to 6
- conv_weight: bfloat16 [32, 4, 5120], P('section'), may hold values from -3 to 3
- beta_logit: float32 [32, 2048, 16], P('section', 'ctx'), may hold values from -12 to 3
- gate_log: float32 [32, 2048, 8], P('section', 'ctx'), may hold values from -2 to 0
- norm_gain: float32 [32, 1024], P('section'), may hold values from 0.25 to 1.75
- w_out: bfloat16 [32, 1024, 2048], P('section', None, 'ctx'), may hold values from -0.1875 to 0.1875
Outputs:
- handed: bfloat16 [32, 2048, 2048], P('section', 'ctx')
All inputs are finite; a program needn't handle non-finite values.
Results may differ from a plain program's by a relative error of at most 0.0049.
Values may be sent and summed in bfloat16 or wider, within the bound.
A program may use at most 128 MiB of HBM per device.

v0:
```python
import jax
import jax.numpy as jnp
from jax import lax
from jax.sharding import PartitionSpec as P

HEAD_TOTAL = 8
HK = 128
STEPS = 2
CONV = 4
SPAN = 128
highest = lax.Precision.HIGHEST


def shifted(value, axis, steps):
    count = lax.axis_size(axis)
    first, last = (max(0, -steps), min(count, count - steps))
    return lax.ppermute(value, axis, [(source, source + steps) for source in range(first, last)])


def entering(value, axis, join, neutral):
    count, mine = (lax.axis_size(axis), lax.axis_index(axis))
    pieces = jax.tree.map(lambda part: lax.all_gather(part, axis), value)
    total = jax.tree.map(
        lambda part, zero: jnp.full_like(part, 0) + jnp.asarray(zero, part.dtype), value, neutral
    )

    def turn(position, total):
        longer = join(total, jax.tree.map(lambda part: part[position], pieces))
        return jax.tree.map(lambda new, old: jnp.where(position < mine, new, old), longer, total)

    return lax.fori_loop(0, count - 1, turn, total)


def passed_along(value, axis, steps):
    count = lax.axis_size(axis)
    pairs = [(source, (source + steps) % count) for source in range(count)]
    return lax.ppermute(value, axis, pairs)


def mix_taps(extended, tap_weights):
    tok_count = extended.shape[0] - tap_weights.shape[0] + 1
    summed = jnp.zeros((tok_count, extended.shape[1]), jnp.float32)
    for offset in range(tap_weights.shape[0]):
        summed = summed + tap_weights[offset].astype(jnp.float32) * extended[
            offset : offset + tok_count
        ].astype(jnp.float32)
    return jax.nn.silu(summed)


def unit_rows(vectors):
    return vectors * lax.rsqrt(jnp.sum(vectors * vectors, axis=-1, keepdims=True) + 1e-06)


def head_major(active, beta_logit, gate_log):
    tok_count = active.shape[0]
    head_width = HEAD_TOTAL * HK
    queries = unit_rows(active[:, :head_width].reshape(tok_count, HEAD_TOTAL, HK)).transpose(
        1, 0, 2
    )
    keys_all = unit_rows(
        active[:, head_width : (1 + STEPS) * head_width].reshape(tok_count, STEPS, HEAD_TOTAL, HK)
    )
    keys_all = keys_all.transpose(2, 0, 1, 3).reshape(HEAD_TOTAL, tok_count * STEPS, HK)
    values_all = active[:, (1 + STEPS) * head_width :].reshape(tok_count, STEPS, HEAD_TOTAL, HK)
    values_all = values_all.transpose(2, 0, 1, 3).reshape(HEAD_TOTAL, tok_count * STEPS, HK)
    step_size = (
        jax.nn.sigmoid(beta_logit.reshape(tok_count, STEPS, HEAD_TOTAL))
        .transpose(2, 0, 1)
        .reshape(HEAD_TOTAL, tok_count * STEPS)
    )
    opening = (lax.broadcasted_iota(jnp.int32, (1, STEPS, 1), 1) == 0).astype(gate_log.dtype)
    log_gate = (
        (gate_log[:, None, :] * opening).transpose(2, 0, 1).reshape(HEAD_TOTAL, tok_count * STEPS)
    )
    return (queries, keys_all, values_all, step_size, log_gate)


def span_terms(queries, keys_all, values_all, step_size, log_gate):
    head_count, virtual, head_dim = keys_all.shape
    blocks = virtual // SPAN
    per_block = SPAN // STEPS
    queries = queries.reshape(head_count, blocks, per_block, head_dim)
    keys_all = keys_all.reshape(head_count, blocks, SPAN, head_dim)
    values_all = values_all.reshape(head_count, blocks, SPAN, head_dim)
    step_size = step_size.reshape(head_count, blocks, SPAN)
    cumulate = jnp.cumsum(log_gate.reshape(head_count, blocks, SPAN), axis=-1)
    query_log = cumulate[..., STEPS - 1 :: STEPS]
    row_index = lax.broadcasted_iota(jnp.int32, (SPAN, SPAN), 0)
    col_index = lax.broadcasted_iota(jnp.int32, (SPAN, SPAN), 1)
    strict = col_index < row_index
    spread = cumulate[..., :, None] - cumulate[..., None, :]
    damping = jnp.where(strict, jnp.exp(jnp.where(strict, spread, 0.0)), 0.0)
    key_inner = jnp.einsum("hcid,hcjd->hcij", keys_all, keys_all, precision=highest)
    unit_lower = (
        jnp.eye(SPAN, dtype=key_inner.dtype) + step_size[..., :, None] * damping * key_inner
    )
    right_sides = jnp.concatenate(
        [step_size[..., None] * values_all, (step_size * jnp.exp(cumulate))[..., None] * keys_all],
        axis=-1,
    )
    solved = jax.scipy.linalg.solve_triangular(
        unit_lower, right_sides, lower=True, unit_diagonal=True
    )
    value_part = solved[..., :head_dim]
    key_part = solved[..., head_dim:]
    to_end = keys_all * jnp.exp(cumulate[..., -1:] - cumulate)[..., None]
    carried = jnp.exp(cumulate[..., -1])[..., None, None] * jnp.eye(head_dim, dtype=key_inner.dtype)
    carried = carried - jnp.einsum("hcid,hcie->hcde", to_end, key_part, precision=highest)
    written = jnp.einsum("hcid,hcie->hcde", to_end, value_part, precision=highest)
    query_row = lax.broadcasted_iota(jnp.int32, (per_block, SPAN), 0) * STEPS + STEPS - 1
    query_col = lax.broadcasted_iota(jnp.int32, (per_block, SPAN), 1)
    allowed = query_col <= query_row
    query_spread = query_log[..., :, None] - cumulate[..., None, :]
    query_damping = jnp.where(allowed, jnp.exp(jnp.where(allowed, query_spread, 0.0)), 0.0)
    scores = jnp.einsum("hcpd,hcid->hcpi", queries, keys_all, precision=highest) * query_damping
    direct = jnp.einsum("hcpi,hcie->hcpe", scores, value_part, precision=highest)
    reach_map = queries * jnp.exp(query_log)[..., None] - jnp.einsum(
        "hcpi,hcie->hcpe", scores, key_part, precision=highest
    )
    return (
        jnp.moveaxis(carried, 1, 0),
        jnp.moveaxis(written, 1, 0),
        jnp.moveaxis(direct, 1, 0),
        jnp.moveaxis(reach_map, 1, 0),
    )


def advance(state_now, piece_terms):
    carried, written, direct, reach_map = piece_terms
    span_out = direct + jnp.einsum("hpd,hde->hpe", reach_map, state_now, precision=highest)
    state_now = jnp.einsum("hde,hef->hdf", carried, state_now, precision=highest) + written
    return (state_now, span_out)


def normalize(outputs, norm_gain):
    tok_count = outputs.shape[0]
    inverse_rms = lax.rsqrt(jnp.mean(outputs * outputs, axis=-1, keepdims=True) + 1e-05)
    return (
        (outputs * inverse_rms * norm_gain.reshape(HEAD_TOTAL, HK))
        .reshape(tok_count, HEAD_TOTAL * HK)
        .astype(jnp.bfloat16)
    )


def combine_pairs(earlier_pair, later_pair):
    first_map, first_add = earlier_pair
    second_map, second_add = later_pair
    joined_map = jnp.einsum("hde,hef->hdf", second_map, first_map, precision=highest)
    joined_add = jnp.einsum("hde,hef->hdf", second_map, first_add, precision=highest) + second_add
    return (joined_map, joined_add)


def compose_step(carried_in, piece_terms):
    so_far, added_state = carried_in
    next_map = jnp.einsum("hde,hef->hdf", piece_terms[0], so_far, precision=highest)
    next_add = (
        jnp.einsum("hde,hef->hdf", piece_terms[0], added_state, precision=highest) + piece_terms[1]
    )
    return ((next_map, next_add), None)


def on_device(streams, conv_weight, beta_logit, gate_log, norm_gain, w_out):
    own_rows = streams[0]
    tok_count = own_rows.shape[0]
    rim_rows = shifted(own_rows[tok_count - (CONV - 1) :], "ctx", 1)
    active = mix_taps(jnp.concatenate([rim_rows, own_rows], axis=0), conv_weight[0])
    span_parts = span_terms(*head_major(active, beta_logit[0], gate_log[0]))
    identity_map = jnp.broadcast_to(jnp.eye(HK, dtype=jnp.float32), (HEAD_TOTAL, HK, HK))
    nothing = jnp.zeros((HEAD_TOTAL, HK, HK), jnp.float32)
    (total_map, total_add), _ = lax.scan(compose_step, (identity_map, nothing), span_parts)
    _, incoming = entering((total_map, total_add), "ctx", combine_pairs, (identity_map, nothing))
    _, outputs = lax.scan(advance, incoming, span_parts)
    outputs = outputs.transpose(0, 2, 1, 3).reshape(tok_count, HEAD_TOTAL, HK)
    normed = normalize(outputs, norm_gain[0])
    local_cols = w_out[0]
    mixed_rows = jnp.dot(
        normed,
        lax.all_gather(local_cols, "ctx", axis=1, tiled=True),
        preferred_element_type=jnp.float32,
    ).astype(jnp.bfloat16)
    return passed_along(mixed_rows[None], "section", 1)


def solution(mesh):
    placed = (
        P("section", "ctx", None),
        P("section", None, None),
        P("section", "ctx", None),
        P("section", "ctx", None),
        P("section", None),
        P("section", None, "ctx"),
    )
    return jax.shard_map(
        on_device, mesh=mesh, in_specs=placed, out_specs=P("section", "ctx", None), check_vma=False
    )
```

profile of v0, /device:TPU:32, one launch (start us, length us, event | category | flops | bytes accessed | tf_op | source)
XLA Modules:
  0.0 527.9 jit_solution(1281271470755481892)
XLA Ops:
  6.5 1.0 slice_bitcast_fusion.3
  7.6 3.8 collective-permute-start
  11.4 1.0 slice_convert_fusion.3
  12.4 0.8 copy.80
  13.6 0.6 reduce_window_sum.11
  14.3 0.7 divide_bitcast_fusion
  15.6 0.6 collective-permute-done
  16.3 1.8 divide_multiply_fusion
  18.5 1.1 copy-done.6
  19.6 0.4 multiply_reduce_fusion
  20.1 0.3 multiply_bitcast_fusion
  20.5 0.5 copy.83
  21.2 1.5 copy.89
  22.7 2.4 fusion.43
  25.1 157.9 %custom-call.4 = f32[8,2,1,128,128]{3,4,2,1,0:T(8,128)} custom-call(f32[8,2,1,128,128]{4,3,2,1,0:T(8,128)S(1)} %fusion.43), custom_call_target="InvertDiagBlocksLowerTriangular" | custom-call | tf_op jit(solution)/shard_map/jit(_solve_triangular)/vmap(vmap())/triangular_solve | solution.py:101
  183.0 1.9 broadcast_multiply_fusion
  184.9 2.0 fusion.35
  186.9 2.2 convolution_bitcast_fusion
  189.3 2.2 fusion.39
  191.7 2.9 while.40
  191.7 0.6 convolution_add_fusion.7
  192.4 0.7 fusion.94
  193.2 0.6 convolution_add_fusion.7
  193.9 0.7 fusion.94
  194.6 0.8 copy-done.2
  195.5 0.6 all-gather.9.cloned.1.call-update
  196.1 0.3 all-gather.11.cloned.1.call-start
  196.4 0.5 all-gather.11.cloned.1.call-update
  197.2 1.2 slice_bitcast_fusion.2
  198.5 0.2 multiply_reduce_fusion.2
  198.7 0.2 multiply_bitcast_fusion.1
  199.0 2.1 convolution_multiply_fusion.1
  201.2 1.9 convolution_bitcast_fusion.2
  203.0 1.1 fusion.46
  204.1 97.6 %all-gather.7.cloned.1.call-done = f32[128,128,128]{2,1,0:T(8,128)} async-done(((f32[8,128,128]{2,1,0:T(8,128)}), f32[128,128,128]{2,1,0:T(8,128)}) %all-gather.7.cloned.1.call-update) | async-done | bytes 8388624 | tf_op jit(solution)/shard_map/all_gather | solution.py:22
  301.7 105.9 %all-gather.9.cloned.1.call-done = f32[128,128,128]{2,1,0:T(8,128)} async-done(((f32[8,128,128]{2,1,0:T(8,128)}), f32[128,128,128]{2,1,0:T(8,128)}) %all-gather.9.cloned.1.call-update) | async-done | bytes 8388624 | tf_op jit(solution)/shard_map/all_gather | solution.py:22
  407.6 29.2 %while.41 = (s32[]{:T(128)}, f32[8,128,128]{2,1,0:T(8,128)S(1)}, s32[]{:T(128)}, f32[16,8,128,128]{3,2,1,0:T(8,128)}, f32[16,8,128,128]{3,2,1,0:T(8,128)}, /*index=5*/s32[]{:T(128)}, s32[]{:T(128)}) while((s32[]{:T(128)}, f32[8,128,128]{2,1,0:T(8,128)S(1)}, s32[]{:T(128)}, f32[16,8,128,128]{3,2,1,0:T(8,128)}, ...), condition=%wide.region_5.6_spmd.clone, body=%wide.region_4.5_spmd.clone.sunk | while | flops 201850880 | bytes 3672671 | solution.py:31
  407.6 1.9 fusion.97
  409.6 1.9 fusion.97
  411.5 1.9 fusion.97
  413.5 1.9 fusion.97
  415.4 1.9 fusion.97
  417.4 1.9 fusion.97
  419.3 1.9 fusion.97
  421.3 1.9 fusion.97
  423.2 1.9 fusion.97
  425.2 1.9 fusion.97
  427.1 1.9 fusion.97
  429.1 1.9 fusion.97
  431.0 1.9 fusion.97
  433.0 1.9 fusion.97
  434.9 1.9 fusion.97
  436.8 6.0 %while.39 = (s32[]{:T(128)}, f32[8,128,128]{2,1,0:T(8,128)S(1)}, f32[2,8,64,128]{3,2,1,0:T(8,128)}, f32[2,8,128,128]{3,2,1,0:T(8,128)S(1)}, f32[2,8,128,128]{3,2...) while((s32[]{:T(128)}, f32[8,128,128]{2,1,0:T(8,128)S(1)}, ...), condition=%wide.region_8.9_spmd, body=%wide.region_7.8_spmd.sunk | while | flops 302186496 | bytes 4458581 | solution.py:172
  436.9 2.3 fusion.89
  439.2 0.6 convolution_add_fusion.6
  439.9 2.3 fusion.89
  442.1 0.6 convolution_add_fusion.6
  442.8 1.3 multiply_reduce_fusion.1
  444.2 1.4 copy.105
  445.5 58.0 %all-gather.11.cloned.1.call-done = bf16[1,1024,2048]{2,1,0:T(8,128)(2,1)} async-done(((bf16[1,1024,128]{2,1,0:T(8,128)(2,1)}), bf16[1,1024,2048]{2,1,0:T(8,128)(2,1)}) %all-gather.11.cloned.1.call-update) | async-done | bytes 4194320 | tf_op jit(solution)/shard_map/all_gather | solution.py:178
  503.7 3.0 fusion.32
  506.7 1.9 collective-permute-start.1
  508.7 11.9 %collective-permute-done.1 = bf16[1,128,2048]{2,1,0:T(8,128)(2,1)S(1)} collective-permute-done((bf16[1,128,2048]{2,1,0:T(8,128)(2,1)S(1)}, bf16[1,128,2048]{2,1,0:T(8,128)(2,1)S(1)}, u32[]{:S(2)}, u32[]{:S(2)}) %collective-permute-start.1) | collective-permute-done | bytes 524320 | tf_op jit(solution)/shard_map/ppermute | solution.py:37
  520.5 0.8 copy.160
  (83 shorter events, 3.7 us)
Async XLA Ops:
  6.5 9.7 %copy-start.7 = (bf16[1,128,5120]{2,1,0:T(8,128)(2,1)S(1)}, bf16[1,128,5120]{2,1,0:T(8,128)(2,1)}, u32[]{:S(2)}) copy-start(bf16[1,128,5120]{2,1,0:T(8,128)(2,1)} %param.12) | copy-start | bytes 3932164
  6.5 295.1 %all-gather.7.cloned.1.call-start = ((), (), s32[]{:S(2)}) async-start(), calls=%async_computation | async-start | bytes 8912896 | tf_op jit(solution)/shard_map/all_gather | solution.py:22
  7.6 8.7 %collective-permute-start = (bf16[3,5120]{1,0:T(4,128)(2,1)S(1)}, bf16[3,5120]{1,0:T(4,128)(2,1)S(1)}, u32[]{:S(2)}, u32[]{:S(2)}) collective-permute-start(bf16[3,5120]{1,0:T(4,128)(2,1)S(1)} %slice_bitcast_fusion.3), channel_id=1, source_target_pairs={{0,1},{1,2},{2,3},{3,4},{4,5},{5,6},{6,7},{7,8},{8,9},{9,10},{10,1... | collective-permute-start | bytes 92168 | tf_op jit(solution)/shard_map/ppermute | solution.py:17
  18.1 1.5 copy-start.6
  21.0 168.3 %copy-start = (f32[8,128,2,128]{3,2,1,0:T(2,128)}, f32[8,128,2,128]{3,2,1,0:T(2,128)S(1)}, u32[]{:S(2)}) copy-start(f32[8,128,2,128]{3,2,1,0:T(2,128)S(1)} %copy.83) | copy-start | bytes 3145732
  183.0 1.9 copy-start.8
  186.9 2.3 copy-start.3
  194.5 0.8 copy-start.2
  194.5 1.0 copy-start.5
  195.4 212.2 %all-gather.9.cloned.1.call-start = ((), (), s32[]{:S(2)}) async-start(), calls=%async_computation.1 | async-start | bytes 8912896 | tf_op jit(solution)/shard_map/all_gather | solution.py:22
  196.1 307.4 %all-gather.11.cloned.1.call-start = ((), (), s32[]{:S(2)}) async-start(), calls=%async_computation.2 | async-start | bytes 4456448 | tf_op jit(solution)/shard_map/all_gather | solution.py:178
  197.1 1.9 copy-start.1
  198.5 2.7 copy-start.4
  436.8 66.9 %copy-start.9 = (f32[1,1024]{1,0:T(1,128)S(1)}, f32[1,1024]{1,0:T(1,128)}, u32[]{:S(2)}) copy-start(f32[1,1024]{1,0:T(1,128)} %param.16) | copy-start | bytes 12292
  506.7 13.8 %collective-permute-start.1 = (bf16[1,128,2048]{2,1,0:T(8,128)(2,1)S(1)}, bf16[1,128,2048]{2,1,0:T(8,128)(2,1)S(1)}, u32[]{:S(2)}, u32[]{:S(2)}) collective-permute-start(bf16[1,128,2048]{2,1,0:T(8,128)(2,1)S(1)} %fusion.32), channel_id=1, source_target_pairs={{0,16},{16,32},{32,48},{48,64},{64,80},{80,96},{96,112},{112,128},... | collective-permute-start | bytes 1572872 | tf_op jit(solution)/shard_map/ppermute | solution.py:37
Sparse Core Ops, SparseCore 0:
  195.5 106.1 all-gather.6
  303.8 103.7 all-gather.8
  409.6 93.8 all-gather.10
where the time goes:
time: 529 us; the launch traced here: 528 us
  waiting for transfers between devices  275 us (52%)
  other arithmetic  167 us (32%)
  matrix products  53.5 us (10%)
  between operations  13.6 us (3%)
  local copies, waits for them, and re-layouts  12.2 us (2%)
  starting transfers between devices  6.05 us (1%)
    all_gather x2, waiting for transfers between devices, entering(): pieces = jax.tree.map(lambda part: lax.all_gather(part, axis), value)  203 us
    another operation x2, other arithmetic, span_terms(): jax.scipy.linalg.solve_triangular(unit_lower, right_sides, lower=True, un...  158 us
    all_gather x1, waiting for transfers between devices, on_device(): lax.all_gather(local_cols, 'ctx', axis=1, tiled=True)  58 us
    dot_general x15, matrix products, combine_pairs(): jnp.einsum('hde,hef->hdf', second_map, first_add, precision=highest)  28.1 us
    ppermute x1, waiting for transfers between devices, passed_along(): return lax.ppermute(value, axis, pairs)  11.9 us
  transfers between devices with their start and end apart: 5, of which 5 were waited for; matrix products, arithmetic and copies ran while one was open for 9% of the time, Pallas kernels for 0%

commit v1 on v0

--- a/solution.py
+++ b/solution.py
@@ -173,10 +173,19 @@
     outputs = outputs.transpose(0, 2, 1, 3).reshape(tok_count, HEAD_TOTAL, HK)
     normed = normalize(outputs, norm_gain[0])
     local_cols = w_out[0]
+
+    def spread_leaf(x0):
+        nodes = lax.psum(1, axis_name="ctx")
+        return lax.all_to_all(
+            jnp.tile(x0, [nodes if dev_j == 1 else 1 for dev_j in range(x0.ndim)]),
+            "ctx",
+            tiled=True,
+            concat_axis=1,
+            split_axis=1,
+        )
+
     mixed_rows = jnp.dot(
-        normed,
-        lax.all_gather(local_cols, "ctx", axis=1, tiled=True),
-        preferred_element_type=jnp.float32,
+        normed, spread_leaf(local_cols), preferred_element_type=jnp.float32
     ).astype(jnp.bfloat16)
     return passed_along(mixed_rows[None], "section", 1)
 

time: 529 us -> 650 us (1.23)
  the two profiles are of different devices: /device:TPU:32 before, /device:TPU:8 now
where the time goes in v1:
time: 650 us; the launch traced here: 648 us
  waiting for transfers between devices  371 us (57%)
  other arithmetic  168 us (26%)
  matrix products  54.2 us (8%)
  starting transfers between devices  20.4 us (3%)
  local copies, waits for them, and re-layouts  19.8 us (3%)
  between operations  13.9 us (2%)
    all_to_all x1, waiting for transfers between devices, spread_leaf(): lax.all_to_all(jnp.tile(x0, [nodes if dev_j == 1 else 1 for dev_j in rang...  221 us
    another operation x2, other arithmetic, span_terms(): jax.scipy.linalg.solve_triangular(unit_lower, right_sides, lower=True, un...  158 us
    all_gather x2, waiting for transfers between devices, entering(): pieces = jax.tree.map(lambda part: lax.all_gather(part, axis), value)  139 us
    dot_general x15, matrix products, combine_pairs(): jnp.einsum('hde,hef->hdf', second_map, first_add, precision=highest)  28.1 us
    all_to_all x1, starting transfers between devices, spread_leaf(): lax.all_to_all(jnp.tile(x0, [nodes if dev_j == 1 else 1 for dev_j in rang...  14.4 us
  transfers between devices with their start and end apart: 5, of which 4 were waited for; matrix products, arithmetic and copies ran while one was open for 3% of the time, Pallas kernels for 0%

profile of v1, /device:TPU:8, one launch (start us, length us, event | category | flops | bytes accessed | tf_op | source)
XLA Modules:
  0.0 648.5 jit_solution(3131241090048343996)
XLA Ops:
  6.5 1.0 slice_bitcast_fusion.3
  7.6 3.8 collective-permute-start
  11.4 1.0 slice_convert_fusion.3
  12.4 0.8 copy.80
  13.6 0.6 reduce_window_sum.11
  14.3 0.7 divide_bitcast_fusion
  15.6 1.8 divide_multiply_fusion
  17.8 1.2 copy-done.6
  19.0 0.4 multiply_reduce_fusion
  19.5 0.3 multiply_bitcast_fusion
  19.8 0.5 copy.83
  20.6 1.5 copy.89
  22.1 2.4 fusion.36
  24.5 157.9 %custom-call.4 = f32[8,2,1,128,128]{3,4,2,1,0:T(8,128)} custom-call(f32[8,2,1,128,128]{4,3,2,1,0:T(8,128)S(1)} %fusion.36), custom_call_target="InvertDiagBlocksLowerTriangular" | custom-call | tf_op jit(solution)/shard_map/jit(_solve_triangular)/vmap(vmap())/triangular_solve | solution.py:101
  182.4 1.9 broadcast_multiply_fusion
  184.3 2.0 fusion.28
  186.3 2.2 convolution_bitcast_fusion
  188.7 2.2 fusion.32
  191.1 2.9 while.40
  191.1 0.6 convolution_add_fusion.7
  191.8 0.7 fusion.89
  192.5 0.6 convolution_add_fusion.7
  193.2 0.7 fusion.89
  193.9 0.8 copy-done.2
  194.8 2.8 tile.9
  197.5 14.4 %all-to-all-start = ((bf16[1024,16,128]{2,0,1:T(8,128)(2,1)}), bf16[1024,16,128]{2,0,1:T(8,128)(2,1)}, u32[]{:S(2)}, u32[]{:S(2)}) async-start(bf16[1024,16,128]{2,0,1:T(8,128)(2,1)} %tile.9), calls=%async_computation | async-start | bytes 8388608 | tf_op jit(solution)/shard_map/all_to_all | solution.py:179
  211.9 0.3 all-gather.7.cloned.1.call-start
  212.1 0.5 all-gather.7.cloned.1.call-update
  213.0 1.2 slice_bitcast_fusion.2
  214.3 0.2 multiply_reduce_fusion.1
  214.8 2.1 convolution_multiply_fusion.1
  217.0 1.9 convolution_bitcast_fusion.2
  218.9 1.1 fusion.39
  219.9 220.9 %all-to-all-done = bf16[1024,16,128]{2,0,1:T(8,128)(2,1)} async-done(((bf16[1024,16,128]{2,0,1:T(8,128)(2,1)}), bf16[1024,16,128]{2,0,1:T(8,128)(2,1)}, u32[]{:S(2)}, u32[]{:S(2)}) %all-to-all-start) | async-done | bytes 4194336 | tf_op jit(solution)/shard_map/all_to_all | solution.py:179
  440.8 6.4 copy.106
  447.3 32.8 %all-gather.5.cloned.1.call-done = f32[128,128,128]{2,1,0:T(8,128)} async-done(((f32[8,128,128]{2,1,0:T(8,128)}), f32[128,128,128]{2,1,0:T(8,128)}) %all-gather.5.cloned.1.call-update) | async-done | bytes 8388624 | tf_op jit(solution)/shard_map/all_gather | solution.py:22
  480.0 106.6 %all-gather.7.cloned.1.call-done = f32[128,128,128]{2,1,0:T(8,128)} async-done(((f32[8,128,128]{2,1,0:T(8,128)}), f32[128,128,128]{2,1,0:T(8,128)}) %all-gather.7.cloned.1.call-update) | async-done | bytes 8388624 | tf_op jit(solution)/shard_map/all_gather | solution.py:22
  586.6 29.2 %while.41 = (s32[]{:T(128)}, f32[8,128,128]{2,1,0:T(8,128)S(1)}, s32[]{:T(128)}, f32[16,8,128,128]{3,2,1,0:T(8,128)}, f32[16,8,128,128]{3,2,1,0:T(8,128)}, /*index=5*/s32[]{:T(128)}, s32[]{:T(128)}) while((s32[]{:T(128)}, f32[8,128,128]{2,1,0:T(8,128)S(1)}, s32[]{:T(128)}, f32[16,8,128,128]{3,2,1,0:T(8,128)}, ...), condition=%wide.region_5.6_spmd.clone, body=%wide.region_4.5_spmd.clone.sunk | while | flops 201850880 | bytes 3672671 | solution.py:31
  586.7 1.9 fusion.92
  588.6 1.9 fusion.92
  590.6 1.9 fusion.92
  592.5 1.9 fusion.92
  594.5 1.9 fusion.92
  596.4 1.9 fusion.92
  598.3 1.9 fusion.92
  600.3 1.9 fusion.92
  602.2 1.9 fusion.92
  604.2 1.9 fusion.92
  606.1 1.9 fusion.92
  608.1 1.9 fusion.92
  610.0 1.9 fusion.92
  612.0 1.9 fusion.92
  613.9 1.9 fusion.92
  615.8 5.9 while.39
  615.9 2.3 fusion.84
  618.2 0.6 convolution_add_fusion.6
  618.9 2.3 fusion.84
  621.1 0.6 convolution_add_fusion.6
  621.8 1.2 fusion.47
  623.1 1.2 fusion.49
  624.5 3.7 fusion.27
  628.2 1.9 collective-permute-start.1
  630.1 10.7 %collective-permute-done.1 = bf16[1,128,2048]{2,1,0:T(8,128)(2,1)S(1)} collective-permute-done((bf16[1,128,2048]{2,1,0:T(8,128)(2,1)S(1)}, bf16[1,128,2048]{2,1,0:T(8,128)(2,1)S(1)}, u32[]{:S(2)}, u32[]{:S(2)}) %collective-permute-start.1) | collective-permute-done | bytes 524320 | tf_op jit(solution)/shard_map/ppermute | solution.py:37
  640.8 0.8 copy.156
  (85 shorter events, 3.6 us)
Async XLA Ops:
  6.5 9.1 %copy-start.7 = (bf16[1,128,5120]{2,1,0:T(8,128)(2,1)S(1)}, bf16[1,128,5120]{2,1,0:T(8,128)(2,1)}, u32[]{:S(2)}) copy-start(bf16[1,128,5120]{2,1,0:T(8,128)(2,1)} %param.12) | copy-start | bytes 3932164
  6.5 473.5 %all-gather.5.cloned.1.call-start = ((), (), s32[]{:S(2)}) async-start(), calls=%async_computation.1 | async-start | bytes 8912896 | tf_op jit(solution)/shard_map/all_gather | solution.py:22
  7.6 8.1 %collective-permute-start = (bf16[3,5120]{1,0:T(4,128)(2,1)S(1)}, bf16[3,5120]{1,0:T(4,128)(2,1)S(1)}, u32[]{:S(2)}, u32[]{:S(2)}) collective-permute-start(bf16[3,5120]{1,0:T(4,128)(2,1)S(1)} %slice_bitcast_fusion.3), channel_id=1, source_target_pairs={{0,1},{1,2},{2,3},{3,4},{4,5},{5,6},{6,7},{7,8},{8,9},{9,10},{10,1... | collective-permute-start | bytes 92168 | tf_op jit(solution)/shard_map/ppermute | solution.py:17
  17.4 1.5 copy-start.6
  20.4 168.3 %copy-start = (f32[8,128,2,128]{3,2,1,0:T(2,128)}, f32[8,128,2,128]{3,2,1,0:T(2,128)S(1)}, u32[]{:S(2)}) copy-start(f32[8,128,2,128]{3,2,1,0:T(2,128)S(1)} %copy.83) | copy-start | bytes 3145732
  182.3 1.9 copy-start.8
  186.3 2.3 copy-start.3
  191.1 3.7 copy-start.9
  193.9 0.8 copy-start.2
  193.9 3.6 copy-start.5
  197.5 243.3 %all-to-all-start = ((bf16[1024,16,128]{2,0,1:T(8,128)(2,1)}), bf16[1024,16,128]{2,0,1:T(8,128)(2,1)}, u32[]{:S(2)}, u32[]{:S(2)}) async-start(bf16[1024,16,128]{2,0,1:T(8,128)(2,1)} %tile.9), calls=%async_computation | async-start | bytes 8388608 | tf_op jit(solution)/shard_map/all_to_all | solution.py:179
  211.9 374.7 %all-gather.7.cloned.1.call-start = ((), (), s32[]{:S(2)}) async-start(), calls=%async_computation.2 | async-start | bytes 8912896 | tf_op jit(solution)/shard_map/all_gather | solution.py:22
  212.9 1.9 copy-start.1
  214.2 2.7 copy-start.4
  615.8 7.2 %copy-start.10 = (f32[1,1024]{1,0:T(1,128)S(1)}, f32[1,1024]{1,0:T(1,128)}, u32[]{:S(2)}) copy-start(f32[1,1024]{1,0:T(1,128)} %param.16) | copy-start | bytes 12292
  628.2 12.6 %collective-permute-start.1 = (bf16[1,128,2048]{2,1,0:T(8,128)(2,1)S(1)}, bf16[1,128,2048]{2,1,0:T(8,128)(2,1)S(1)}, u32[]{:S(2)}, u32[]{:S(2)}) collective-permute-start(bf16[1,128,2048]{2,1,0:T(8,128)(2,1)S(1)} %fusion.27), channel_id=1, source_target_pairs={{0,16},{16,32},{32,48},{48,64},{64,80},{80,96},{96,112},{112,128},... | collective-permute-start | bytes 1572872 | tf_op jit(solution)/shard_map/ppermute | solution.py:37
Sparse Core Ops, SparseCore 0:
  194.9 285.1 all-gather.4
  482.1 104.4 all-gather.6
